TPU v7x, 128 devices: a whole 4x4x4 slice. The times are simulated.
128 devices in a mesh: vert: 64 (over z, y_hi, x, core), row: 2 (over y_lo).
Axes of the slice: x: 4, y: 4 (y_hi: 2, y_lo: 2; y = y_hi * 2 + y_lo), z: 4, core: 2. Of those that a mesh axis runs over, the one named last changes fastest.
Arguments:
- features: float32 [524288, 256], P(('vert', 'row')), may hold values from -6 to 6
- w_self: float32 [256, 256], replicated, may hold values from -0.375 to 0.375
- w_neigh: float32 [256, 256], replicated, may hold values from -0.75 to 0.75
- bias: float32 [256], replicated, may hold values from -3 to 3
- w_head: float32 [256], replicated, may hold values from -0.75 to 0.75
- tile_weights: float32 [16384, 128, 128], P(('vert', 'row')), may hold values from 0.01 to 1
- tile_dst: int32 [16384], P(('vert', 'row')), may hold values from 0 to 31
- tile_src: int32 [16384], P(('vert', 'row')), may hold values from 0 to 167
- tile_count: int32 [128], P(('vert', 'row')), may hold values from 16 to 128, as said below
- hub_block: int32 [128], P(('vert', 'row')), may hold values from 0 to 31
- send_rows: int32 [128, 128, 8], P(('vert', 'row')), may hold values from 0 to 4095
- send_count: int32 [128, 128], P(('vert', 'row')), may hold values from 1 to 8, as said below
- labels: int32 [524288], P(('vert', 'row')), may hold values from 0 to 1
Outputs:
- grad_self: float32 [256, 256], replicated
- grad_neigh: float32 [256, 256], replicated
- grad_bias: float32 [256], replicated
- grad_head: float32 [256], replicated
Inputs may be any that keep to these rules, and one draw needn't show every extreme that they name: Tile t of a device is used when t < its tile_count; some device uses all 128 tiles and some 128 // 8. `send_count`: each sending device fills all 8 slots for at least one receiving device.
All inputs are finite; a program needn't handle non-finite values.
Results may differ from a plain program's by a relative error of at most 0.0003.
Values sent between devices are 32-bit elements; how exact they have to be, the bound alone decides.
A program may use at most 128 MiB of HBM per device.

v0:
```python
import math
import jax
import jax.numpy as jnp
from jax import lax
from jax.sharding import PartitionSpec as P

FULL_PRECISION = lax.Precision.HIGHEST


def on_device(
    features,
    w_self,
    w_neigh,
    bias,
    w_head,
    tile_weights,
    tile_dst,
    tile_src,
    tile_count,
    hub_block,
    send_rows,
    send_count,
    labels,
):
    tile_size = tile_weights.shape[1]
    tile_total = tile_weights.shape[0]
    feature_width = features.shape[1]
    block_count = features.shape[0] // tile_size
    slot_count = send_rows.shape[2]
    own_blocks = features.reshape(block_count, tile_size, feature_width)
    hub_local = lax.dynamic_slice_in_dim(own_blocks, hub_block[0], 1, 0)
    hub_blocks = lax.all_gather(hub_local, ("vert", "row"), axis=0, tiled=True)
    outgoing = features[send_rows[0]]
    slot_index = jnp.arange(slot_count, dtype=jnp.int32)
    alive = slot_index[None, :] < send_count[0][:, None]
    outgoing = jnp.where(alive[:, :, None], outgoing, jnp.zeros_like(outgoing))
    incoming = lax.all_to_all(outgoing, ("vert", "row"), split_axis=0, concat_axis=0, tiled=True)
    source_table = jnp.concatenate(
        [own_blocks, incoming.reshape(-1, tile_size, feature_width), hub_blocks], 0
    )
    active = jnp.arange(tile_total, dtype=jnp.int32) < tile_count[0]
    picked = source_table[tile_src]
    contrib = jnp.einsum("tij,tjf->tif", tile_weights, picked, precision=FULL_PRECISION)
    block_ids = jnp.arange(block_count, dtype=jnp.int32)
    selector = ((tile_dst[None, :] == block_ids[:, None]) & active[None, :]).astype(features.dtype)
    summed = jnp.einsum("bt,tif->bif", selector, contrib, precision=FULL_PRECISION)
    weight_sum = jnp.einsum(
        "bt,ti->bi", selector, jnp.sum(tile_weights, axis=2), precision=FULL_PRECISION
    )
    neigh_mean = ((own_blocks + summed) / (1.0 + weight_sum)[:, :, None]).reshape(-1, feature_width)
    pre_act = (
        jnp.dot(features, w_self, precision=FULL_PRECISION)
        + jnp.dot(neigh_mean, w_neigh, precision=FULL_PRECISION)
        + bias[None, :]
    )
    sigmoid_pre = jax.nn.sigmoid(pre_act)
    hidden = pre_act * sigmoid_pre
    head_score = jnp.dot(hidden, w_head, precision=FULL_PRECISION)
    target = 2.0 * labels.astype(features.dtype) - 1.0
    vertex_total = features.shape[0] * lax.axis_size(("vert", "row"))
    loss_scale = 1.0 / math.sqrt(vertex_total)
    dscore = (head_score - target) * loss_scale
    dpre = dscore[:, None] * w_head[None, :] * (sigmoid_pre * (1.0 + pre_act * (1.0 - sigmoid_pre)))
    local_self = jnp.dot(features.T, dpre, precision=FULL_PRECISION)
    local_neigh = jnp.dot(neigh_mean.T, dpre, precision=FULL_PRECISION)
    local_bias = jnp.sum(dpre, axis=0)
    local_head = jnp.dot(hidden.T, dscore, precision=FULL_PRECISION)
    grad_self, grad_neigh, grad_bias, grad_head = lax.psum(
        (local_self, local_neigh, local_bias, local_head), ("vert", "row")
    )
    return (grad_self, grad_neigh, grad_bias, grad_head)


def solution(mesh):
    in_specs = (
        P(("vert", "row"), None),
        P(),
        P(),
        P(),
        P(),
        P(("vert", "row"), None, None),
        P(("vert", "row")),
        P(("vert", "row")),
        P(("vert", "row")),
        P(("vert", "row")),
        P(("vert", "row"), None, None),
        P(("vert", "row"), None),
        P(("vert", "row")),
    )
    out_specs = (P(), P(), P(), P())
    return jax.shard_map(
        on_device, mesh=mesh, in_specs=in_specs, out_specs=out_specs, check_vma=False
    )
```

profile of v0, /device:TPU:1, one launch (start us, length us, event | category | flops | bytes accessed | tf_op | source)
XLA Modules:
  0.0 630.4 jit_solution(8257241849353653896)
XLA Ops:
  7.9 1.6 constant_dynamic-slice_fusion
  10.4 5.7 gather_fusion
  16.2 1.2 bitcast_select_fusion
  17.4 11.5 %all-to-all-start = ((f32[128,8,256]{2,1,0:T(8,128)}), f32[128,8,256]{2,1,0:T(8,128)S(1)}, u32[]{:S(2)}, u32[]{:S(2)}) async-start(f32[128,8,256]{2,1,0:T(8,128)} %bitcast_select_fusion), calls=%async_computation | async-start | bytes 2097152 | tf_op jit(solution)/shard_map/all_to_all | solution.py:37
  29.6 5.6 reduce_sum.18
  35.6 7.6 %fusion.21 = f32[4096,256]{1,0:T(8,128)} fusion(f32[4096,256]{1,0:T(8,128)} %param.13, f32[256,256]{1,0:T(8,128)S(1)} %copy-done), kind=kOutput, calls=%fused_computation.41 | convolution fusion | flops 3221225472 | bytes 8650752 | tf_op jit(solution)/shard_map/dot_general | solution.py:52
  43.2 8.0 %all-to-all-done = f32[128,8,256]{2,1,0:T(8,128)S(1)} async-done(((f32[128,8,256]{2,1,0:T(8,128)}), f32[128,8,256]{2,1,0:T(8,128)S(1)}, u32[]{:S(2)}, u32[]{:S(2)}) %all-to-all-start) | async-done | bytes 1048608 | tf_op jit(solution)/shard_map/all_to_all | solution.py:37
  51.2 294.8 %all-gather.2.cloned.1.call-done = f32[128,128,256]{2,1,0:T(8,128)} async-done(((f32[1,128,256]{2,1,0:T(8,128)}), f32[128,128,256]{2,1,0:T(8,128)}) %all-gather.2.cloned.1.call-update) | async-done | bytes 16777232 | tf_op jit(solution)/shard_map/all_gather | solution.py:32
  346.0 15.9 %pad_maximum_fusion = f32[168,128,256]{2,1,0:T(8,128)} fusion(f32[128,128,256]{2,1,0:T(8,128)} %all-gather.2.cloned.1.call-done, f32[8,128,256]{2,1,0:T(8,128)S(1)} %bitcast.58, f32[32,128,256]{2,1,0:T(8,128)} %bitcast.54), kind=kLoop, calls=%fused_computation.2 | loop fusion | flops 11010048 | bytes 44040192 | tf_op jit(solution)/shard_map/concatenate | solution.py:38
  362.0 17.3 %gather_fusion.1 = f32[128,128,256]{2,1,0:T(8,128)} fusion(f32[168,128,256]{2,1,0:T(8,128)} %pad_maximum_fusion, s32[1024]{0:T(1024)S(1)} %pad_clamp_fusion), kind=kCustom, calls=%fused_computation.1 | custom fusion | bytes 33554944 | tf_op jit(solution)/shard_map/gather | solution.py:42
  379.3 34.3 %convolution_bitcast_fusion = f32[128,128,256]{1,2,0:T(8,128)} fusion(f32[128,128,256]{2,1,0:T(8,128)} %gather_fusion.1, f32[128,128,128]{2,1,0:T(8,128)} %param.18), kind=kOutput, calls=%fused_computation.3 | convolution fusion | flops 6442450944 | bytes 41943040 | tf_op jit(solution)/shard_map/tij,tjf->tif/dot_general | solution.py:43
  413.6 17.7 %copy.26 = f32[128,128,256]{2,0,1:T(8,128)} copy(f32[128,128,256]{1,2,0:T(8,128)} %convolution_bitcast_fusion) | data formatting | bytes 33554432 | tf_op jit(solution)/shard_map/tij,tjf->tif/dot_general | solution.py:43
  431.2 13.7 %fusion.4 = f32[32,128,256]{2,0,1:T(8,128)S(1)} fusion(f32[32,128,256]{2,1,0:T(8,128)} %bitcast.55, f32[128,128,256]{2,0,1:T(8,128)} %copy.26, f32[32,128]{0,1:T(8,128)S(1)} %copy.28, s32[128]{0:T(128)S(1)} %copy-done.7, pred[128]{0:T(512)(128)(4,1)S(1)} %iota_compare_fusion.2), kind=kOutput, calls=%fused_computation.12 | convolution fusion | flops 1612718080 | bytes 25182848 | tf_op jit(solution)/shard_map/bt,tif->bif/dot_general | solution.py:46
  445.0 2.4 copy.29
  447.5 3.4 fusion
  450.9 4.4 fusion.5
  455.4 2.4 fusion.20
  457.9 7.5 %fusion.22 = f32[256,256]{1,0:T(8,128)} fusion(f32[4096,256]{1,0:T(8,128)S(1)} %bitcast.57, f32[4096,256]{1,0:T(8,128)S(1)} %get-tuple-element.21), kind=kOutput, calls=%fused_computation.42 | convolution fusion | flops 3221225472 | bytes 8650752 | tf_op jit(solution)/shard_map/dot_general | solution.py:65
  465.4 7.7 %convolution_bitcast_fusion.1 = f32[256,256]{0,1:T(8,128)} fusion(f32[4096,256]{1,0:T(8,128)S(1)} %get-tuple-element.21, f32[4096,256]{1,0:T(8,128)S(1)} %copy-done.2), kind=kOutput, calls=%fused_computation.20 | convolution fusion | flops 3221225472 | bytes 8650752 | tf_op jit(solution)/shard_map/dot_general | solution.py:64
  473.1 5.2 fusion.7
  478.2 67.7 %all-reduce = (f32[256]{0:T(256)}, f32[256]{0:T(256)}) all-reduce(f32[256]{0:T(256)S(1)} %get-tuple-element.20, f32[256]{0:T(256)S(1)} %bitcast.62), channel_id=1, replica_groups=mesh['vert'=64,'row'=2] {'vert','row'}, use_global_device_ids=true, to_apply=%region_4.5 | all-reduce | flops 512 | bytes 4096 | tf_op jit(solution)/shard_map/psum | solution.py:68
  545.9 74.0 %all-reduce.4.cloned.1.call-done = (f32[256,256]{0,1:T(8,128)}, f32[256,256]{1,0:T(8,128)}) async-done(((f32[256,256]{0,1:T(8,128)}, f32[256,256]{1,0:T(8,128)}), (f32[256,256]{0,1:T(8,128)}, f32[256,256]{1,0:T(8,128)})) %all-reduce.4.cloned.1.call-update) | async-done | bytes 524304 | tf_op jit(solution)/shard_map/psum | solution.py:68
  619.9 1.8 copy.30
  621.7 1.7 copy.39
  (39 shorter events, 1.5 us)
Async XLA Ops:
  7.2 28.4 %copy-start = (f32[256,256]{1,0:T(8,128)S(1)}, f32[256,256]{1,0:T(8,128)}, u32[]{:S(2)}) copy-start(f32[256,256]{1,0:T(8,128)} %param.14) | copy-start | bytes 786436
  7.2 338.9 %all-gather.2.cloned.1.call-start = ((), (), s32[]{:S(2)}) async-start(), calls=%async_computation.1 | async-start | bytes 16908288 | tf_op jit(solution)/shard_map/all_gather | solution.py:32
  10.4 5.7 copy-start.10
  17.4 33.8 %all-to-all-start = ((f32[128,8,256]{2,1,0:T(8,128)}), f32[128,8,256]{2,1,0:T(8,128)S(1)}, u32[]{:S(2)}, u32[]{:S(2)}) async-start(f32[128,8,256]{2,1,0:T(8,128)} %bitcast_select_fusion), calls=%async_computation | async-start | bytes 2097152 | tf_op jit(solution)/shard_map/all_to_all | solution.py:37
  28.9 591.0 %all-reduce.4.cloned.1.call-start = ((), (), s32[]{:S(2)}) async-start(), calls=%async_computation.2 | async-start | bytes 1048576 | tf_op jit(solution)/shard_map/psum | solution.py:68
  29.6 5.7 copy-start.7
  29.6 5.9 copy-start.11
  445.0 2.5 copy-start.4
  445.0 2.5 copy-start.5
  445.0 2.5 copy-start.8
  447.5 3.5 copy-start.9
  450.9 4.5 copy-start.3
  450.9 4.5 copy-start.6
  457.9 7.5 %copy-start.2 = (f32[4096,256]{1,0:T(8,128)S(1)}, f32[4096,256]{1,0:T(8,128)}, u32[]{:S(2)}) copy-start(f32[4096,256]{1,0:T(8,128)} %param.13) | copy-start | bytes 12582916
  473.1 150.3 %copy-start.1 = (f32[256,256]{1,0:T(8,128)S(1)}, f32[256,256]{1,0:T(8,128)}, u32[]{:S(2)}) copy-start(f32[256,256]{1,0:T(8,128)} %param.14) | copy-start | bytes 786436
Sparse Core Ops, SparseCore 0:
  10.3 335.7 all-gather.1
  473.2 146.6 all-reduce.3
where the time goes:
time: 636 us; the launch traced here: 630 us
  waiting for transfers between devices  377 us (59%)
  matrix products  83.9 us (13%)
  blocking collectives  67.7 us (11%)
  local copies, waits for them, and re-layouts  48.4 us (8%)
  other arithmetic  26 us (4%)
  between operations  15.9 us (2%)
  starting transfers between devices  11.6 us (2%)
    all_gather x1, waiting for transfers between devices, on_device(): hub_blocks = lax.all_gather(hub_local, ('vert', 'row'), axis=0, tiled=True)  295 us
    psum x1, waiting for transfers between devices, on_device(): lax.psum((local_self, local_neigh, local_bias, local_head), ('vert', 'row'))  74 us
    psum x1, blocking collectives, on_device(): lax.psum((local_self, local_neigh, local_bias, local_head), ('vert', 'row'))  67.7 us
    dot_general x1, matrix products, on_device(): jnp.einsum('tij,tjf->tif', tile_weights, picked, precision=FULL_PRECISION)  34.3 us
    dot_general x1, local copies, waits for them, and re-layouts, on_device(): jnp.einsum('tij,tjf->tif', tile_weights, picked, precision=FULL_PRECISION)  17.7 us
    gather x1, local copies, waits for them, and re-layouts, on_device(): picked = source_table[tile_src]  17.3 us
    concatenate x1, other arithmetic, on_device(): jnp.concatenate([own_blocks, incoming.reshape(-1, tile_size, feature_widt...  15.9 us
    dot_general x1, matrix products, on_device(): jnp.einsum('bt,tif->bif', selector, contrib, precision=FULL_PRECISION)  13.7 us
  transfers between devices with their start and end apart: 3, of which 3 were waited for; matrix products, arithmetic and copies ran while one was open for 4% of the time, Pallas kernels for 0%

commit v1 on v0

--- a/solution.py
+++ b/solution.py
@@ -29,7 +29,12 @@
     slot_count = send_rows.shape[2]
     own_blocks = features.reshape(block_count, tile_size, feature_width)
     hub_local = lax.dynamic_slice_in_dim(own_blocks, hub_block[0], 1, 0)
-    hub_blocks = lax.all_gather(hub_local, ("vert", "row"), axis=0, tiled=True)
+    hub_blocks = jnp.concatenate(
+        lax.all_to_all(
+            jnp.stack([hub_local] * lax.axis_size(("vert", "row"))), ("vert", "row"), 0, 0
+        ),
+        axis=0,
+    )
     outgoing = features[send_rows[0]]
     slot_index = jnp.arange(slot_count, dtype=jnp.int32)
     alive = slot_index[None, :] < send_count[0][:, None]

time: 636 us -> 579 us (0.910)
  waiting for transfers between devices: 377 us -> 301 us
  local copies, waits for them, and re-layouts: 48.4 us -> 55.6 us
    all_gather x1 -> x0, waiting for transfers between devices: 295 us -> none  [on_device(): hub_blocks = lax.all_gather(hub_local, ('vert', 'row'), axis=0, tiled=True)]
    all_to_all x0 -> x1, waiting for transfers between devices: none -> 207 us  [on_device(): lax.all_to_all(jnp.stack([hub_local] * lax.axis_size(('vert', 'row'))), (...]
    all_to_all x1, waiting for transfers between devices: 8.03 us -> 18.1 us  [on_device(): lax.all_to_all(outgoing, ('vert', 'row'), split_axis=0, concat_axis=0, ti...]
    another operation x0 -> x1, local copies, waits for them, and re-layouts: none -> 7.83 us  [on_device(): jnp.stack([hub_local] * lax.axis_size(('vert', 'row')))]
  transfers between devices with their start and end apart: 3 -> 3, of which waited for: 3 -> 3; matrix products, arithmetic and copies ran while one was open for 4% -> 3% of each run, Pallas kernels for 0% -> 0%
where the time goes in v1:
time: 579 us; the launch traced here: 571 us
  waiting for transfers between devices  301 us (52%)
  matrix products  83.9 us (14%)
  blocking collectives  71.5 us (12%)
  local copies, waits for them, and re-layouts  55.6 us (10%)
  other arithmetic  26.8 us (5%)
  starting transfers between devices  16.5 us (3%)
  between operations  15.8 us (3%)
    all_to_all x1, waiting for transfers between devices, on_device(): lax.all_to_all(jnp.stack([hub_local] * lax.axis_size(('vert', 'row'))), (...  207 us
    psum x1, waiting for transfers between devices, on_device(): lax.psum((local_self, local_neigh, local_bias, local_head), ('vert', 'row'))  76.1 us
    psum x1, blocking collectives, on_device(): lax.psum((local_self, local_neigh, local_bias, local_head), ('vert', 'row'))  71.5 us
    dot_general x1, matrix products, on_device(): jnp.einsum('tij,tjf->tif', tile_weights, picked, precision=FULL_PRECISION)  34.3 us
    all_to_all x1, waiting for transfers between devices, on_device(): lax.all_to_all(outgoing, ('vert', 'row'), split_axis=0, concat_axis=0, ti...  18.1 us
    dot_general x1, local copies, waits for them, and re-layouts, on_device(): jnp.einsum('tij,tjf->tif', tile_weights, picked, precision=FULL_PRECISION)  17.7 us
    gather x1, local copies, waits for them, and re-layouts, on_device(): picked = source_table[tile_src]  17.3 us
    concatenate x1, other arithmetic, on_device(): jnp.concatenate([own_blocks, incoming.reshape(-1, tile_size, feature_widt...  16.1 us
  transfers between devices with their start and end apart: 3, of which 3 were waited for; matrix products, arithmetic and copies ran while one was open for 3% of the time, Pallas kernels for 0%

profile of v1, /device:TPU:1, one launch (start us, length us, event | category | flops | bytes accessed | tf_op | source)
XLA Modules:
  0.0 571.5 jit_solution(11468503422854393280)
XLA Ops:
  8.9 5.7 gather_fusion
  15.7 11.5 %all-to-all-start = ((f32[128,8,256]{2,1,0:T(8,128)}), f32[128,8,256]{2,1,0:T(8,128)S(1)}, u32[]{:S(2)}, u32[]{:S(2)}) async-start(f32[128,8,256]{2,1,0:T(8,128)} %bitcast_select_fusion), calls=%async_computation | async-start | bytes 2097152 | tf_op jit(solution)/shard_map/all_to_all | solution.py:42
  28.8 18.1 %all-to-all-done = f32[128,8,256]{2,1,0:T(8,128)S(1)} async-done(((f32[128,8,256]{2,1,0:T(8,128)}), f32[128,8,256]{2,1,0:T(8,128)S(1)}, u32[]{:S(2)}, u32[]{:S(2)}) %all-to-all-start) | async-done | bytes 1048608 | tf_op jit(solution)/shard_map/all_to_all | solution.py:42
  46.9 7.8 %stack.2 = f32[128,1,128,256]{3,2,1,0:T(8,128)} broadcast(f32[128,256]{1,0:T(8,128)S(1)} %dynamic-slice_bitcast_fusion), dimensions={2,3} | broadcast | bytes 16908288 | tf_op jit(solution)/shard_map/stack | solution.py:34
  54.7 5.0 all-to-all-start.1
  60.5 5.6 reduce_sum.18
  66.4 7.6 %fusion.25 = f32[4096,256]{1,0:T(8,128)} fusion(f32[4096,256]{1,0:T(8,128)} %param.13, f32[256,256]{1,0:T(8,128)S(1)} %copy-done), kind=kOutput, calls=%fused_computation.42 | convolution fusion | flops 3221225472 | bytes 8650752 | tf_op jit(solution)/shard_map/dot_general | solution.py:57
  74.0 206.9 %all-to-all-done.1 = f32[128,1,128,256]{3,2,1,0:T(8,128)} async-done(((f32[128,1,128,256]{3,2,1,0:T(8,128)}), f32[128,1,128,256]{3,2,1,0:T(8,128)}, u32[]{:S(2)}, u32[]{:S(2)}) %all-to-all-start.1) | async-done | bytes 16777248 | tf_op jit(solution)/shard_map/all_to_all | solution.py:33
  280.9 16.1 %pad_maximum_fusion = f32[168,128,256]{2,1,0:T(8,128)} fusion(f32[128,128,256]{2,1,0:T(8,128)} %bitcast.9, f32[8,128,256]{2,1,0:T(8,128)S(1)} %bitcast.63, f32[32,128,256]{2,1,0:T(8,128)} %bitcast.59), kind=kLoop, calls=%fused_computation.2 | loop fusion | flops 11010048 | bytes 44040192 | tf_op jit(solution)/shard_map/concatenate | solution.py:43
  297.0 17.3 %gather_fusion.1 = f32[128,128,256]{2,1,0:T(8,128)} fusion(f32[168,128,256]{2,1,0:T(8,128)} %pad_maximum_fusion, s32[1024]{0:T(1024)S(1)} %pad_clamp_fusion), kind=kCustom, calls=%fused_computation.1 | custom fusion | bytes 33554944 | tf_op jit(solution)/shard_map/gather | solution.py:47
  314.3 34.3 %fusion.26 = f32[128,256,128]{2,1,0:T(8,128)} fusion(f32[128,128,256]{2,1,0:T(8,128)} %gather_fusion.1, f32[128,128,128]{2,1,0:T(8,128)} %param.18), kind=kOutput, calls=%fused_computation.43 | convolution fusion | flops 6442450944 | bytes 41943040 | tf_op jit(solution)/shard_map/tij,tjf->tif/dot_general | solution.py:48
  348.6 17.7 %copy.25 = f32[128,256,128]{1,0,2:T(8,128)} copy(f32[128,256,128]{2,1,0:T(8,128)} %fusion.26) | data formatting | bytes 33554432 | tf_op jit(solution)/shard_map/tij,tjf->tif/dot_general | solution.py:48
  366.3 13.7 %fusion.6 = f32[32,128,256]{2,0,1:T(8,128)S(1)} fusion(f32[32,128,256]{2,1,0:T(8,128)} %bitcast.60, f32[32,128]{0,1:T(8,128)S(1)} %copy.22, f32[128,256,128]{1,0,2:T(8,128)} %copy.25, s32[128]{0:T(128)S(1)} %copy-done.7, pred[128]{0:T(512)(128)(4,1)S(1)} %iota_compare_fusion.2), kind=kOutput, calls=%fused_computation.13 | convolution fusion | flops 1612718080 | bytes 25182848 | tf_op jit(solution)/shard_map/bt,tif->bif/dot_general | solution.py:51
  380.1 2.4 copy.23
  382.6 3.4 fusion.2
  386.0 4.4 fusion.7
  390.5 2.4 fusion.24
  393.0 7.5 %fusion.27 = f32[256,256]{1,0:T(8,128)} fusion(f32[4096,256]{1,0:T(8,128)S(1)} %bitcast.62, f32[4096,256]{1,0:T(8,128)S(1)} %get-tuple-element.17), kind=kOutput, calls=%fused_computation.44 | convolution fusion | flops 3221225472 | bytes 8650752 | tf_op jit(solution)/shard_map/dot_general | solution.py:70
  400.4 7.7 %convolution_bitcast_fusion = f32[256,256]{0,1:T(8,128)} fusion(f32[4096,256]{1,0:T(8,128)S(1)} %get-tuple-element.17, f32[4096,256]{1,0:T(8,128)S(1)} %copy-done.2), kind=kOutput, calls=%fused_computation.21 | convolution fusion | flops 3221225472 | bytes 8650752 | tf_op jit(solution)/shard_map/dot_general | solution.py:69
  408.1 5.2 fusion.9
  413.3 71.5 %all-reduce = (f32[256]{0:T(256)}, f32[256]{0:T(256)}) all-reduce(f32[256]{0:T(256)S(1)} %get-tuple-element.16, f32[256]{0:T(256)S(1)} %bitcast.67), channel_id=1, replica_groups=mesh['vert'=64,'row'=2] {'vert','row'}, use_global_device_ids=true, to_apply=%region_4.5 | all-reduce | flops 512 | bytes 4096 | tf_op jit(solution)/shard_map/psum | solution.py:73
  484.8 76.1 %all-reduce.4.cloned.1.call-done = (f32[256,256]{0,1:T(8,128)}, f32[256,256]{1,0:T(8,128)}) async-done(((f32[256,256]{0,1:T(8,128)}, f32[256,256]{1,0:T(8,128)}), (f32[256,256]{0,1:T(8,128)}, f32[256,256]{1,0:T(8,128)})) %all-reduce.4.cloned.1.call-update) | async-done | bytes 524304 | tf_op jit(solution)/shard_map/psum | solution.py:73
  560.9 1.8 copy.24
  562.7 1.7 copy.33
  (37 shorter events, 4.2 us)
Async XLA Ops:
  7.2 59.3 %copy-start = (f32[256,256]{1,0:T(8,128)S(1)}, f32[256,256]{1,0:T(8,128)}, u32[]{:S(2)}) copy-start(f32[256,256]{1,0:T(8,128)} %param.14) | copy-start | bytes 786436
  15.7 31.2 %all-to-all-start = ((f32[128,8,256]{2,1,0:T(8,128)}), f32[128,8,256]{2,1,0:T(8,128)S(1)}, u32[]{:S(2)}, u32[]{:S(2)}) async-start(f32[128,8,256]{2,1,0:T(8,128)} %bitcast_select_fusion), calls=%async_computation | async-start | bytes 2097152 | tf_op jit(solution)/shard_map/all_to_all | solution.py:42
  54.7 226.2 %all-to-all-start.1 = ((f32[128,1,128,256]{3,2,1,0:T(8,128)}), f32[128,1,128,256]{3,2,1,0:T(8,128)}, u32[]{:S(2)}, u32[]{:S(2)}) async-start(f32[128,1,128,256]{3,2,1,0:T(8,128)} %stack.2), calls=%async_computation.1 | async-start | bytes 33554432 | tf_op jit(solution)/shard_map/all_to_all | solution.py:33
  59.8 501.2 %all-reduce.4.cloned.1.call-start = ((), (), s32[]{:S(2)}) async-start(), calls=%async_computation.2 | async-start | bytes 1048576 | tf_op jit(solution)/shard_map/psum | solution.py:73
  60.5 5.7 copy-start.7
  60.5 5.9 %copy-start.10 = (s32[128]{0:T(128)S(1)}, s32[128]{0:T(128)}, u32[]{:S(2)}) copy-start(s32[128]{0:T(128)} %param.20) | copy-start | bytes 1540
  380.0 2.5 copy-start.4
  380.1 2.5 copy-start.5
  380.1 2.5 copy-start.8
  382.5 3.5 copy-start.9
  386.0 4.5 copy-start.3
  386.0 4.5 copy-start.6
  393.0 7.5 %copy-start.2 = (f32[4096,256]{1,0:T(8,128)S(1)}, f32[4096,256]{1,0:T(8,128)}, u32[]{:S(2)}) copy-start(f32[4096,256]{1,0:T(8,128)} %param.13) | copy-start | bytes 12582916
  408.1 156.3 %copy-start.1 = (f32[256,256]{1,0:T(8,128)S(1)}, f32[256,256]{1,0:T(8,128)}, u32[]{:S(2)}) copy-start(f32[256,256]{1,0:T(8,128)} %param.14) | copy-start | bytes 786436
Sparse Core Ops, SparseCore 0:
  408.3 152.6 all-reduce.3
